TPU v7x, 32 devices: a whole 2x2x4 slice. The times are simulated.
32 devices in a mesh: groups: 2 (over y), seq: 4 (over z), head: 4 (over x, core).
Axes of the slice: x: 2, y: 2, z: 4, core: 2. Of those that a mesh axis runs over, the one named last changes fastest.
Arguments:
- query: bfloat16 [16, 1024, 128], P('head', ('groups', 'seq')), parts along dimension 1, may hold values from -400 to 400
- keys: bfloat16 [4, 1024, 128], P('head', ('groups', 'seq')), parts along dimension 1, may hold values from -5 to 5
- values: bfloat16 [4, 1024, 128], P('head', ('groups', 'seq')), parts along dimension 1, may hold values from -6 to 6
- ratio: bfloat16 [16, 1024, 128], P('head', ('groups', 'seq')), parts along dimension 1, may hold values from -4 to 4
- block_order: int32 [16], P('groups'), parts along dimension 0, may hold values from 0 to 7, each once
Outputs:
- query_rel: float32 [16, 1024, 128], P('head', ('groups', 'seq')), parts along dimension 1
- key_rel: float32 [4, 1024, 128], P('head', ('groups', 'seq')), parts along dimension 1
- value_rel: float32 [4, 1024, 128], P('head', ('groups', 'seq')), parts along dimension 1
There are 2 independent parts, one for each index of `groups`. A program takes and returns all parts, laid end to end along the dimension named above; each array names one. Nothing has to cross between parts.
Inputs may be any that keep to these rules, and one draw needn't show every extreme that they name: A permutation: stored block b holds prompt block block_order[b], each once.
All inputs are finite; a program needn't handle non-finite values.
Results may differ from a plain program's by a relative error of at most 0.04.
Values may be sent and summed in bfloat16 or wider, within the bound.
No kernel may reach another device: no remote copies, remote signals or barrier semaphores. Data moves between devices by JAX's collectives and lax.ppermute only.
A program may use at most 64 MiB of HBM per device.

v0:
```python
import math

import jax
import jax.numpy as jnp
from jax import lax
from jax.sharding import PartitionSpec as P


def block_width(row_total):
    return math.gcd(row_total, 512)


def token_places(block_order, block_rows):
    offsets = jnp.arange(block_rows, dtype=jnp.int32)
    return (block_order[:, None] * block_rows + offsets[None, :]).reshape(-1)


def scores_of(query_rows, query_places, key_block, key_places, score_scale):
    scores = (
        jnp.einsum("qd,kd->qk", query_rows, key_block, preferred_element_type=jnp.float32)
        * score_scale
    )
    return jnp.where(key_places[None, :] <= query_places[:, None], scores, -jnp.inf)


def row_stats(query_rows, ratio_rows, query_places, key_all, value_all, key_places, score_scale):
    block_size = block_width(key_all.shape[0])
    row_count = query_rows.shape[0]

    def row_advance(step_index, loop_state):
        first_row = step_index * block_size
        key_block = lax.dynamic_slice_in_dim(key_all, first_row, block_size, 0)
        value_block = lax.dynamic_slice_in_dim(value_all, first_row, block_size, 0)
        block_places = lax.dynamic_slice_in_dim(key_places, first_row, block_size, 0)
        row_top, row_total, weighted = loop_state
        scores = scores_of(query_rows, query_places, key_block, block_places, score_scale)
        new_top = jnp.maximum(row_top, jnp.max(scores, axis=1))
        shrink = jnp.exp(row_top - new_top)
        exp_scores = jnp.exp(scores - new_top[:, None])
        prob_grad = jnp.einsum(
            "qd,kd->qk", ratio_rows, value_block, preferred_element_type=jnp.float32
        )
        return (
            new_top,
            row_total * shrink + jnp.sum(exp_scores, axis=1),
            weighted * shrink + jnp.sum(exp_scores * prob_grad, axis=1),
        )

    start_state = (
        jnp.full((row_count,), -1e30, jnp.float32),
        jnp.zeros((row_count,), jnp.float32),
        jnp.zeros((row_count,), jnp.float32),
    )
    row_top, row_total, weighted = lax.fori_loop(
        0, key_all.shape[0] // block_size, row_advance, start_state
    )
    return (row_top, row_total, weighted / row_total)


def block_grads(
    query_rows, ratio_rows, query_places, stats, key_block, value_block, key_places, score_scale
):
    row_top, row_total, row_expect = stats
    scores = scores_of(query_rows, query_places, key_block, key_places, score_scale)
    weights = jnp.exp(scores - row_top[:, None]) / row_total[:, None]
    prob_grad = jnp.einsum("qd,kd->qk", ratio_rows, value_block, preferred_element_type=jnp.float32)
    soft_grad = (weights * (prob_grad - row_expect[:, None])).astype(jnp.bfloat16)
    return (soft_grad, weights.astype(jnp.bfloat16))


def side_terms(soft_grad, low_weights, query_rows, ratio_rows):
    key_part = jnp.einsum("qk,qd->kd", soft_grad, query_rows, preferred_element_type=jnp.float32)
    value_part = jnp.einsum(
        "qk,qd->kd", low_weights, ratio_rows, preferred_element_type=jnp.float32
    )
    return jnp.concatenate((key_part, value_part), axis=1)


def query_pass(
    query_rows, ratio_rows, query_places, stats, key_all, value_all, key_places, score_scale
):
    block_size = block_width(key_all.shape[0])
    head_size = key_all.shape[1]

    def query_advance(step_index, loop_state):
        first_row = step_index * block_size
        key_block = lax.dynamic_slice_in_dim(key_all, first_row, block_size, 0)
        value_block = lax.dynamic_slice_in_dim(value_all, first_row, block_size, 0)
        block_places = lax.dynamic_slice_in_dim(key_places, first_row, block_size, 0)
        query_sum, term_table = loop_state
        soft_grad, low_weights = block_grads(
            query_rows,
            ratio_rows,
            query_places,
            stats,
            key_block,
            value_block,
            block_places,
            score_scale,
        )
        query_sum = query_sum + jnp.dot(soft_grad, key_block, preferred_element_type=jnp.float32)
        pieces = side_terms(soft_grad, low_weights, query_rows, ratio_rows)
        term_table = lax.dynamic_update_slice_in_dim(term_table, pieces, first_row, 0)
        return (query_sum, term_table)

    empty_table = jnp.zeros((key_all.shape[0], 2 * head_size), jnp.float32)
    start_state = (jnp.zeros((query_rows.shape[0], head_size), jnp.float32), empty_table)
    return lax.fori_loop(0, key_all.shape[0] // block_size, query_advance, start_state)


def body(query, keys, values, ratio, block_order):
    kv_heads, tokens_dev, head_size = keys.shape
    group_size = query.shape[0] // kv_heads
    score_scale = head_size ** (-0.5)
    places_all = token_places(block_order, tokens_dev // 2)
    seq_index = lax.axis_index("seq")
    local_places = lax.dynamic_slice_in_dim(places_all, seq_index * tokens_dev, tokens_dev, 0)
    row_places = jnp.tile(local_places, group_size)
    key_all, value_all = (
        lax.all_gather(keys, "seq", axis=1, tiled=True),
        lax.all_gather(values, "seq", axis=1, tiled=True),
    )
    query_list, key_list, value_list = ([], [], [])
    query_rows = query.reshape(group_size * tokens_dev, head_size)
    ratio_rows = ratio.reshape(group_size * tokens_dev, head_size)
    keys_seen = key_all[0]
    values_seen = value_all[0]
    stats = row_stats(
        query_rows, ratio_rows, row_places, keys_seen, values_seen, places_all, score_scale
    )
    query_sum, term_table = query_pass(
        query_rows, ratio_rows, row_places, stats, keys_seen, values_seen, places_all, score_scale
    )

    def term_rows(first_row, row_count, table=term_table):
        return table

    summed = lax.psum_scatter(
        term_rows(jnp.int32(0), lax.axis_size("seq") * tokens_dev),
        "seq",
        scatter_dimension=0,
        tiled=True,
    )
    query_list.append(
        0.5
        * score_scale
        * query.astype(jnp.float32)
        * query_sum.reshape(group_size, tokens_dev, head_size)
    )
    key_list.append(0.5 * score_scale * keys[0].astype(jnp.float32) * summed[:, :head_size])
    value_list.append(values[0].astype(jnp.float32) * summed[:, head_size:])
    return (query_list[0], jnp.stack(key_list, axis=0), jnp.stack(value_list, axis=0))


def solution(mesh):
    return jax.shard_map(
        body,
        mesh=mesh,
        in_specs=(
            P("head", ("groups", "seq"), None),
            P("head", ("groups", "seq"), None),
            P("head", ("groups", "seq"), None),
            P("head", ("groups", "seq"), None),
            P("groups"),
        ),
        out_specs=(
            P("head", ("groups", "seq"), None),
            P("head", ("groups", "seq"), None),
            P("head", ("groups", "seq"), None),
        ),
        check_vma=False,
    )
```

profile of v0, /device:TPU:0, one launch (start us, length us, event | category | flops | bytes accessed | tf_op | source)
XLA Modules:
  0.0 71.9 jit_solution(825619412379754486)
XLA Ops:
  7.2 0.0 copy-start
  7.2 0.0 copy-start.1
  7.2 0.0 reduce-scatter.2.cloned.1.call-start
  7.2 0.0 copy-start.4
  7.2 15.4 %all_gather.6 = bf16[1,512,128]{2,1,0:T(8,128)(2,1)S(1)} all-gather(bf16[1,128,128]{2,1,0:T(8,128)(2,1)} %param.6), channel_id=1, replica_groups=mesh['groups'=2,'seq'=4,'head'=4] {'seq'}, dimensions={1}, use_global_device_ids=true | all-gather | bytes 163840 | tf_op jit(solution)/shard_map/all_gather | solution.py:120
  22.7 0.0 copy-done.4
  22.7 0.1 iota_add_fusion
  22.8 0.1 add.67
  22.8 0.1 dynamic_slice.15
  22.9 0.0 copy-done.1
  22.9 0.0 copy-start.2
  22.9 0.4 fusion.13
  23.3 0.4 copy-done.2
  23.7 13.5 %all_gather.7 = bf16[1,512,128]{2,1,0:T(8,128)(2,1)S(1)} all-gather(bf16[1,128,128]{2,1,0:T(8,128)(2,1)S(1)} %copy-done.2), channel_id=1, replica_groups=mesh['groups'=2,'seq'=4,'head'=4] {'seq'}, dimensions={1}, use_global_device_ids=true | all-gather | bytes 163840 | tf_op jit(solution)/shard_map/all_gather | solution.py:121
  37.2 0.0 copy-done
  37.2 0.4 fusion.2
  37.6 0.4 fusion.3
  38.1 0.3 multiply_convert_fusion
  38.4 0.3 fusion.14
  38.7 0.8 %pad_maximum_fusion = f32[512,256]{0,1:T(8,128)} fusion(f32[512,128]{0,1:T(8,128)S(1)} %fusion.3, f32[512,128]{0,1:T(8,128)S(1)} %fusion.14), kind=kLoop, calls=%fused_computation.8 | loop fusion | flops 131072 | bytes 1048576 | tf_op jit(solution)/shard_map/while/body/eval_jaxpr/concatenate | solution.py:76
  39.5 0.0 reduce-scatter.2.cloned.1.call-update
  39.5 0.0 copy-start.3
  39.5 0.1 copy.9
  39.7 0.6 copy-done.3
  40.3 0.1 copy.8
  40.4 1.0 %convolution_multiply_fusion.1 = f32[4,128,128]{2,1,0:T(8,128)} fusion(bf16[4,128,512]{2,1,0:T(8,128)(2,1)S(1)} %bitcast.35, bf16[4,128,128]{2,1,0:T(8,128)(2,1)S(1)} %copy-done.1, bf16[1,512,128]{2,1,0:T(8,128)(2,1)S(1)} %all_gather.6), kind=kOutput, calls=%fused_computation.2 | convolution fusion | flops 67305472 | bytes 1048576 | tf_op jit(solution)/shard_map/while/body/eval_jaxpr/dot_general | solution.py:101
  41.4 21.3 %reduce-scatter.2.cloned.1.call-done = f32[128,256]{0,1:T(8,128)} async-done(((f32[512,256]{0,1:T(8,128)}), f32[128,256]{0,1:T(8,128)}) %reduce-scatter.2.cloned.1.call-update) | async-done | bytes 131088 | tf_op jit(solution)/shard_map/reduce_scatter | solution.py:138
  62.7 0.9 %fusion.9 = (f32[1,128,128]{1,2,0:T(8,128)S(1)}, f32[1,128,128]{1,2,0:T(8,128)S(1)}) fusion(f32[128,256]{0,1:T(8,128)} %reduce-scatter.2.cloned.1.call-done, bf16[1,128,128]{1,2,0:T(8,128)(2,1)S(1)} %copy.9, bf16[1,128,128]{1,2,0:T(8,128)(2,1)S(1)} %copy.8), kind=kLoop, calls=%fused_computation.16 | loop fusion | flops 81920 | bytes 327680 | tf_op jit(solution)/shard_map/stack | solution.py:152
  63.6 0.7 %copy.10 = f32[1,128,128]{2,1,0:T(8,128)} copy(f32[1,128,128]{1,2,0:T(8,128)S(1)} %get-tuple-element.55) | data formatting | bytes 131072
  64.4 0.7 %copy.11 = f32[1,128,128]{2,1,0:T(8,128)} copy(f32[1,128,128]{1,2,0:T(8,128)S(1)} %get-tuple-element.54) | data formatting | bytes 131072
  (4 shorter events, 0.0 us)
Async XLA Ops:
  7.2 30.0 %copy-start = (bf16[4,128,128]{2,1,0:T(8,128)(2,1)S(1)}, bf16[4,128,128]{2,1,0:T(8,128)(2,1)}, u32[]{:S(2)}) copy-start(bf16[4,128,128]{2,1,0:T(8,128)(2,1)} %param.8) | copy-start | bytes 393220
  7.2 15.7 %copy-start.1 = (bf16[4,128,128]{2,1,0:T(8,128)(2,1)S(1)}, bf16[4,128,128]{2,1,0:T(8,128)(2,1)}, u32[]{:S(2)}) copy-start(bf16[4,128,128]{2,1,0:T(8,128)(2,1)} %param.5) | copy-start | bytes 393220
  7.2 55.5 %reduce-scatter.2.cloned.1.call-start = ((), (), s32[]{:S(2)}) async-start(), calls=%async_computation.1 | async-start | bytes 655360 | tf_op jit(solution)/shard_map/reduce_scatter | solution.py:138
  7.2 15.4 %copy-start.4 = (s32[8]{0:T(128)S(1)}, s32[8]{0:T(128)}, u32[]{:S(2)}) copy-start(s32[8]{0:T(128)} %param.9) | copy-start | bytes 100
  22.9 0.8 %copy-start.2 = (bf16[1,128,128]{2,1,0:T(8,128)(2,1)S(1)}, bf16[1,128,128]{2,1,0:T(8,128)(2,1)}, u32[]{:S(2)}) copy-start(bf16[1,128,128]{2,1,0:T(8,128)(2,1)} %param.7) | copy-start | bytes 98308
  39.5 0.8 %copy-start.3 = (bf16[1,128,128]{2,1,0:T(8,128)(2,1)S(1)}, bf16[1,128,128]{2,1,0:T(8,128)(2,1)}, u32[]{:S(2)}) copy-start(bf16[1,128,128]{2,1,0:T(8,128)(2,1)} %param.6) | copy-start | bytes 98308
Sparse Core Ops, SparseCore 0:
  39.6 23.0 reduce-scatter.1
where the time goes:
time: 72.3 us; the launch traced here: 71.9 us
  blocking collectives  28.9 us (40%)
  waiting for transfers between devices  21.3 us (29%)
  between operations  14.1 us (20%)
  local copies, waits for them, and re-layouts  2.86 us (4%)
  matrix products  2.53 us (3%)
  other arithmetic  2.12 us (3%)
    reduce_scatter x1, waiting for transfers between devices, body(): lax.psum_scatter(term_rows(jnp.int32(0), lax.axis_size('seq') * tokens_de...  21.3 us
    all_gather x1, blocking collectives, body(): lax.all_gather(keys, 'seq', axis=1, tiled=True)  15.4 us
    all_gather x1, blocking collectives, body(): lax.all_gather(values, 'seq', axis=1, tiled=True)  13.5 us
    unnamed x14, local copies, waits for them, and re-layouts  2.7 us
  transfers between devices with their start and end apart: 1, of which 1 were waited for; matrix products, arithmetic and copies ran while one was open for 2% of the time, Pallas kernels for 0%

commit v1 on v0

v1 whole, which is shorter than its diff:
```python
import functools
import math

import jax
import jax.numpy as jnp
from jax import lax
from jax.experimental import pallas as pl
from jax.experimental.pallas import tpu as pltpu
from jax.sharding import PartitionSpec as P

F32 = jnp.float32
BF16 = jnp.bfloat16
HIDDEN = -1e30
FEW = 8
LOG2E = math.log2(math.e)


def dot(a, b, dims):
    return lax.dot_general(a, b, (dims, ((), ())), preferred_element_type=F32)


def each(count, step, unrolled):
    if unrolled:
        for slot in range(count):
            step(slot)
    else:
        lax.fori_loop(0, count, lambda slot, _: (step(slot), None)[1], None)


def main_kernel(
    shape, scale, order_ref, owner_ref, query_ref, ratio_ref, key_ref, value_ref, *rest
):
    slots, blocks, block_rows, joined = shape
    rows = blocks * block_rows
    queries = query_ref.shape[0]
    if joined:
        (seen_ref, terms_ref, soft_ref, score_ref, grad_ref) = rest
    else:
        seen = rest[: slots - 1]
        terms = rest[slots - 1 : 2 * slots - 1]
        soft_ref, score_ref, grad_ref = rest[2 * slots - 1 :]
    head = query_ref.shape[1]

    def keys_of(slot):
        if joined:
            return seen_ref[slot, :, :head]
        return key_ref[...] if slot == 0 else seen[slot - 1][:, :head]

    def values_of(slot):
        if joined:
            return seen_ref[slot, :, head:]
        return value_ref[...] if slot == 0 else seen[slot - 1][:, head:]

    def rows_of(slot):
        return pl.ds(pl.multiple_of(slot * rows, rows), rows)

    lane = lax.broadcasted_iota(jnp.int32, (1, queries), 1) % rows
    mine = owner_ref[slots]
    places = lane % block_rows
    for block in range(blocks):
        first = order_ref[mine * blocks + block] * block_rows
        places = places + jnp.where(lane // block_rows == block, first, 0)
    inner = lax.broadcasted_iota(jnp.int32, (block_rows, queries), 0)

    def scores(slot):
        found = dot(keys_of(slot), query_ref[...], ((1,), (1,)))
        parts = []
        for block in range(blocks):
            first = order_ref[owner_ref[slot] * blocks + block] * block_rows
            part = found[block * block_rows : (block + 1) * block_rows]
            parts.append(jnp.where(inner <= places - first, part, HIDDEN))
        found = jnp.concatenate(parts, axis=0)
        score_ref[rows_of(slot), :] = found
        grad_ref[rows_of(slot), :] = dot(values_of(slot), ratio_ref[...], ((1,), (1,)))
        return jnp.max(found.reshape(rows // 8, 8, queries), axis=0)

    def exps(slot, top):
        power = jnp.exp2((score_ref[rows_of(slot), :] - top) * (scale * LOG2E))
        score_ref[rows_of(slot), :] = power
        weighted = power * grad_ref[rows_of(slot), :]
        return (
            jnp.sum(power.reshape(rows // 8, 8, queries), axis=0),
            jnp.sum(weighted.reshape(rows // 8, 8, queries), axis=0),
        )

    if joined:
        top = lax.fori_loop(
            0,
            slots,
            lambda slot, top: jnp.maximum(top, scores(slot)),
            jnp.full((8, queries), HIDDEN, F32),
        )
    else:
        top = functools.reduce(jnp.maximum, [scores(slot) for slot in range(slots)])
    top = jnp.max(top, axis=0, keepdims=True)
    if joined:
        zero = jnp.zeros((8, queries), F32)

        def add(slot, sums):
            total, weighted = exps(slot, top)
            return sums[0] + total, sums[1] + weighted

        total, weighted = lax.fori_loop(0, slots, add, (zero, zero))
    else:
        sums = [exps(slot, top) for slot in range(slots)]
        total = functools.reduce(jnp.add, [one for one, _ in sums])
        weighted = functools.reduce(jnp.add, [one for _, one in sums])
    share = 1.0 / jnp.sum(total, axis=0, keepdims=True)
    expect = jnp.sum(weighted, axis=0, keepdims=True) * share

    def finish(slot):
        weights = score_ref[rows_of(slot), :] * share
        soft = (weights * (grad_ref[rows_of(slot), :] - expect)).astype(BF16)
        soft_ref[rows_of(slot), :] = soft
        key_part = dot(soft, query_ref[...], ((1,), (0,)))
        value_part = dot(weights.astype(BF16), ratio_ref[...], ((1,), (0,)))
        if joined:
            terms_ref[slot, :, :head] = key_part
            terms_ref[slot, :, head:] = value_part
        else:
            terms[slot][:, :head] = key_part.astype(terms[slot].dtype)
            terms[slot][:, head:] = value_part.astype(terms[slot].dtype)

    if joined:
        each(slots, finish, False)
    else:
        for slot in (*range(1, slots), 0):
            finish(slot)


def query_kernel(shape, factor, query_ref, soft_ref, key_ref, *rest):
    slots, rows, joined = shape
    *seen, out_ref = rest
    head = query_ref.shape[1]

    def part(slot, keys):
        soft = soft_ref[pl.ds(pl.multiple_of(slot * rows, rows), rows), :]
        return dot(soft, keys, ((0,), (0,)))

    if joined:
        out_ref[...] = jnp.zeros_like(out_ref)

        def add(slot):
            out_ref[...] += part(slot, seen[0][slot, :, :head])

        each(slots, add, False)
        found = out_ref[...]
    else:
        found = part(0, key_ref[...])
        for slot in range(1, slots):
            found += part(slot, seen[slot - 1][:, :head])
    out_ref[...] = factor * query_ref[...].astype(F32) * found


def sum_kernel(factor, key_ref, value_ref, own_ref, *rest):
    *got, key_out, value_out = rest
    head = key_ref.shape[1]
    total = own_ref[...]
    for one in got:
        total = total + one[...].astype(F32)
    key_out[...] = factor * key_ref[...].astype(F32) * total[:, :head]
    value_out[...] = value_ref[...].astype(F32) * total[:, head:]


def body(query, keys, values, ratio, block_order):
    kv_heads, rows, head = keys.shape
    group = query.shape[0] // kv_heads
    queries = group * rows
    scale = head ** (-0.5)
    slots = lax.axis_size("seq")
    mine = lax.axis_index("seq")
    blocks = block_order.shape[0] // slots
    block_rows = rows // blocks
    joined = slots > FEW
    swap = slots & (slots - 1) == 0
    limit = min(60 << 20, (8 << 20) + 16 * slots * rows * queries)
    smem = pl.BlockSpec(memory_space=pltpu.SMEM)
    vmem = pl.BlockSpec(memory_space=pltpu.VMEM)

    def partner(step):
        return mine ^ step if swap else lax.rem(mine - step + slots, slots)

    def pairs(step, back):
        if swap:
            return [(device, device ^ step) for device in range(slots)]
        step = -step if back else step
        return [(device, (device + step) % slots) for device in range(slots)]

    def one_head(query_rows, ratio_rows, key_rows, value_rows):
        both = jnp.concatenate((key_rows, value_rows), axis=1)
        if joined:
            owners = jnp.append(jnp.arange(slots, dtype=jnp.int32), mine)
            seen = [lax.all_gather(both, "seq")]
            terms_shape = [jax.ShapeDtypeStruct((slots, rows, 2 * head), F32)]
        else:
            owners = jnp.stack([partner(step) if step else mine for step in range(slots)] + [mine])
            seen = [lax.ppermute(both, "seq", pairs(step, False)) for step in range(1, slots)]
            terms_shape = [
                jax.ShapeDtypeStruct((rows, 2 * head), BF16 if step else F32) for step in range(slots)
            ]
        *terms, soft = pl.pallas_call(
            functools.partial(main_kernel, (slots, blocks, block_rows, joined), scale),
            out_shape=(*terms_shape, jax.ShapeDtypeStruct((slots * rows, queries), BF16)),
            in_specs=[smem, smem] + [vmem] * (4 + len(seen)),
            out_specs=tuple([vmem] * (len(terms_shape) + 1)),
            scratch_shapes=[
                pltpu.VMEM((slots * rows, queries), F32),
                pltpu.VMEM((slots * rows, queries), F32),
            ],
            compiler_params=pltpu.CompilerParams(vmem_limit_bytes=limit),
            cost_estimate=pl.CostEstimate(
                flops=8 * slots * rows * queries * head,
                bytes_accessed=4 * slots * rows * queries,
                transcendentals=slots * rows * queries,
            ),
        )(block_order, owners.astype(jnp.int32), query_rows, ratio_rows, key_rows, value_rows, *seen)
        if joined:
            own = lax.psum_scatter(terms[0], "seq", scatter_dimension=0, tiled=False)
            got = []
        else:
            own = terms[0]
            got = [lax.ppermute(terms[step], "seq", pairs(step, True)) for step in range(1, slots)]
        query_out = pl.pallas_call(
            functools.partial(query_kernel, (slots, rows, joined), 0.5 * scale),
            out_shape=jax.ShapeDtypeStruct((queries, head), F32),
            in_specs=[vmem] * (3 + len(seen)),
            out_specs=vmem,
            compiler_params=pltpu.CompilerParams(vmem_limit_bytes=limit),
            cost_estimate=pl.CostEstimate(
                flops=2 * slots * rows * queries * head,
                bytes_accessed=2 * slots * rows * queries,
                transcendentals=0,
            ),
        )(query_rows, soft, key_rows, *seen)
        key_out, value_out = pl.pallas_call(
            functools.partial(sum_kernel, 0.5 * scale),
            out_shape=(jax.ShapeDtypeStruct((rows, head), F32),) * 2,
            in_specs=[vmem] * (3 + len(got)),
            out_specs=(vmem, vmem),
            compiler_params=pltpu.CompilerParams(vmem_limit_bytes=limit),
        )(key_rows, value_rows, own, *got)
        return query_out.reshape(group, rows, head), key_out, value_out

    results = [
        one_head(
            query[g * group : (g + 1) * group].reshape(queries, head),
            ratio[g * group : (g + 1) * group].reshape(queries, head),
            keys[g],
            values[g],
        )
        for g in range(kv_heads)
    ]
    return (
        jnp.concatenate([one for one, _, _ in results], axis=0),
        jnp.stack([one for _, one, _ in results], axis=0),
        jnp.stack([one for _, _, one in results], axis=0),
    )


def solution(mesh):
    spec = P("head", ("groups", "seq"), None)
    return jax.shard_map(
        body,
        mesh=mesh,
        in_specs=(spec, spec, spec, spec, P("groups")),
        out_specs=(spec, spec, spec),
        check_vma=False,
    )
```

time: 72.3 us -> 27 us (0.37)
  blocking collectives: 28.9 us -> 0 us
  between operations: 14.1 us -> 0.67 us
  waiting for transfers between devices: 21.3 us -> 8.96 us
  starting transfers between devices: 0.04 us -> 10.2 us
  Pallas kernels: 0 us -> 3.57 us
  matrix products: 2.53 us -> 0 us
  other arithmetic: 2.12 us -> 0.83 us
    all_gather x2 -> x0, blocking collectives: 28.9 us -> none  [the longest x1 15.4 us: body(): lax.all_gather(keys, 'seq', axis=1, tiled=True)]
    reduce_scatter x1 -> x0, waiting for transfers between devices: 21.3 us -> none  [body(): lax.psum_scatter(term_rows(jnp.int32(0), lax.axis_size('seq') * tokens_de...]
    ppermute x0 -> x6, starting transfers between devices: none -> 10.2 us  [the longest x3 5.71 us: one_head(): lax.ppermute(both, 'seq', pairs(step, False))]
    ppermute x0 -> x6, waiting for transfers between devices: none -> 8.96 us  [the longest x3 5.99 us: one_head(): lax.ppermute(both, 'seq', pairs(step, False))]
    pallas_call x0 -> x3, Pallas kernels: none -> 3.57 us  [the longest x1 1.85 us: one_head(): pl.pallas_call(functools.partial(main_kernel, (slots, blocks, block_rows,...]
    dot_general x5 -> x0, matrix products: 2.53 us -> none  [the longest x1 1.01 us: query_advance(): jnp.dot(soft_grad, key_block, preferred_element_type=jnp.float32)]
    another operation x1 -> x0, other arithmetic: 0.89 us -> none  [body(): jnp.stack(value_list, axis=0)]
    unnamed x14 -> x10, local copies, waits for them, and re-layouts: 2.7 us -> 2.47 us
  transfers between devices with their start and end apart: 1 -> 6, of which waited for: 1 -> 4; matrix products, arithmetic and copies ran while one was open for 2% -> 0% of each run, Pallas kernels for 0% -> 4%
where the time goes in v1:
time: 27 us; the launch traced here: 26.7 us
  starting transfers between devices  10.2 us (38%)
  waiting for transfers between devices  8.96 us (33%)
  Pallas kernels  3.57 us (13%)
  local copies, waits for them, and re-layouts  2.55 us (9%)
  other arithmetic  0.83 us (3%)
  between operations  0.67 us (2%)
    ppermute x3, waiting for transfers between devices, one_head(): lax.ppermute(both, 'seq', pairs(step, False))  5.99 us
    ppermute x3, starting transfers between devices, one_head(): lax.ppermute(both, 'seq', pairs(step, False))  5.71 us
    ppermute x3, starting transfers between devices, one_head(): lax.ppermute(terms[step], 'seq', pairs(step, True))  4.44 us
    ppermute x3, waiting for transfers between devices, one_head(): lax.ppermute(terms[step], 'seq', pairs(step, True))  2.98 us
    unnamed x10, local copies, waits for them, and re-layouts  2.47 us
    pallas_call x1, Pallas kernels, one_head(): pl.pallas_call(functools.partial(main_kernel, (slots, blocks, block_rows,...  1.85 us
    pallas_call x1, Pallas kernels, one_head(): pl.pallas_call(functools.partial(query_kernel, (slots, rows, joined), 0.5...  1.04 us
    concatenate x1, other arithmetic, one_head(): both = jnp.concatenate((key_rows, value_rows), axis=1)  0.83 us
  transfers between devices with their start and end apart: 6, of which 4 were waited for; matrix products, arithmetic and copies ran while one was open for 0% of the time, Pallas kernels for 4%

profile of v1, /device:TPU:0, one launch (start us, length us, event | category | flops | bytes accessed | tf_op | source)
XLA Modules:
  0.0 26.7 jit_solution(10389215399753830255)
XLA Ops:
  0.6 0.0 copy-start
  0.6 0.0 copy-start.2
  0.7 0.8 %pad_maximum_fusion = bf16[128,256]{1,0:T(8,128)(2,1)S(1)} fusion(bf16[128,128]{1,0:T(8,128)(2,1)} %bitcast.17, bf16[128,128]{1,0:T(8,128)(2,1)} %bitcast.11), kind=kLoop, calls=%fused_computation | loop fusion | flops 131072 | bytes 131072 | tf_op jit(solution)/shard_map/concatenate | solution.py:190
  1.5 3.1 %collective-permute-start = (bf16[128,256]{1,0:T(8,128)(2,1)S(1)}, bf16[128,256]{1,0:T(8,128)(2,1)S(1)}, u32[]{:S(2)}, u32[]{:S(2)}) collective-permute-start(bf16[128,256]{1,0:T(8,128)(2,1)S(1)} %pad_maximum_fusion), channel_id=1, source_target_pairs={{0,4},{4,0},{8,12},{12,8},{1,5},{5,1},{9,13},{13,9},{2,6},{6,2},{1... | collective-permute-start | bytes 196616 | tf_op jit(solution)/shard_map/ppermute | solution.py:197
  4.6 2.6 %collective-permute-start.1 = (bf16[128,256]{1,0:T(8,128)(2,1)S(1)}, bf16[128,256]{1,0:T(8,128)(2,1)S(1)}, u32[]{:S(2)}, u32[]{:S(2)}) collective-permute-start(bf16[128,256]{1,0:T(8,128)(2,1)S(1)} %pad_maximum_fusion), channel_id=1, source_target_pairs={{0,8},{4,12},{8,0},{12,4},{1,9},{5,13},{9,1},{13,5},{2,10},{6,14},... | collective-permute-start | bytes 196616 | tf_op jit(solution)/shard_map/ppermute | solution.py:197
  7.2 0.0 collective-permute-start.2
  7.2 0.1 stack.26.owner_ref
  7.3 0.0 collective-permute-done.rest_0_
  7.3 4.6 %collective-permute-done.1.rest_1_ = bf16[128,256]{1,0:T(8,128)(2,1)S(1)} collective-permute-done((bf16[128,256]{1,0:T(8,128)(2,1)S(1)}, bf16[128,256]{1,0:T(8,128)(2,1)S(1)}, u32[]{:S(2)}, u32[]{:S(2)}) %collective-permute-start.1) | collective-permute-done | bytes 65568 | tf_op jit(solution)/shard_map/ppermute | solution.py:197
  11.9 1.4 %collective-permute-done.2.rest_2_ = bf16[128,256]{1,0:T(8,128)(2,1)S(1)} collective-permute-done((bf16[128,256]{1,0:T(8,128)(2,1)S(1)}, bf16[128,256]{1,0:T(8,128)(2,1)S(1)}, u32[]{:S(2)}, u32[]{:S(2)}) %collective-permute-start.2) | collective-permute-done | bytes 65568 | tf_op jit(solution)/shard_map/ppermute | solution.py:197
  13.3 0.0 copy-start.4
  13.3 0.0 copy-done
  13.3 0.0 copy-done.2
  13.3 0.6 %copy-done.4 = s32[8]{0:T(128)S(1)} copy-done((s32[8]{0:T(128)S(1)}, s32[8]{0:T(128)}, u32[]{:S(2)}) %copy-start.4) | copy-done | bytes 56
  13.9 0.0 copy-start.1
  13.9 0.9 %copy-done.1 = bf16[4,128,128]{2,1,0:T(8,128)(2,1)S(1)} copy-done((bf16[4,128,128]{2,1,0:T(8,128)(2,1)S(1)}, bf16[4,128,128]{2,1,0:T(8,128)(2,1)}, u32[]{:S(2)}) %copy-start.1) | copy-done | bytes 131096
  14.8 0.0 copy-start.3
  14.8 0.9 %copy-done.3 = bf16[4,128,128]{2,1,0:T(8,128)(2,1)S(1)} copy-done((bf16[4,128,128]{2,1,0:T(8,128)(2,1)S(1)}, bf16[4,128,128]{2,1,0:T(8,128)(2,1)}, u32[]{:S(2)}) %copy-start.3) | copy-done | bytes 131096
  15.7 1.8 %shard_map.76 = (f32[128,256]{1,0:T(8,128)S(1)}, bf16[128,256]{1,0:T(8,128)(2,1)S(1)}, bf16[128,256]{1,0:T(8,128)(2,1)S(1)}, bf16[128,256]{1,0:T(8,128)(2,1)S(1)}, bf16[512,512]{1,0:T(8,128)(2,1)S(1)}) custom-call(s32[8]{0:T(128)S(1)} %copy-done.4, s32[5]{0:T(128)S(1)} %stack.26.owner_ref, bf16[512,128]{1,0:T(8,128)(2,1)S(1)} %bitcast.15, ...), custom_call_target="tpu_custom_call" | custom-call | flops 268435456 | bytes 1048576 | tf_op jit(solution)/shard_map/pallas_call | solution.py:201
  17.6 0.1 collective-permute-start.3
  17.7 2.3 %collective-permute-start.4 = (bf16[128,256]{1,0:T(8,128)(2,1)S(1)}, bf16[128,256]{1,0:T(8,128)(2,1)S(1)}, u32[]{:S(2)}, u32[]{:S(2)}) collective-permute-start(bf16[128,256]{1,0:T(8,128)(2,1)S(1)} %get-tuple-element.13), channel_id=1, source_target_pairs={{0,8},{4,12},{8,0},{12,4},{1,9},{5,13},{9,1},{13,5},{2,10},{6,14},... | collective-permute-start | bytes 196616 | tf_op jit(solution)/shard_map/ppermute | solution.py:222
  20.0 2.0 %collective-permute-start.5 = (bf16[128,256]{1,0:T(8,128)(2,1)S(1)}, bf16[128,256]{1,0:T(8,128)(2,1)S(1)}, u32[]{:S(2)}, u32[]{:S(2)}) collective-permute-start(bf16[128,256]{1,0:T(8,128)(2,1)S(1)} %get-tuple-element.14), channel_id=1, source_target_pairs={{0,12},{4,8},{8,4},{12,0},{1,13},{5,9},{9,5},{13,1},{2,14},{6,10},... | collective-permute-start | bytes 196616 | tf_op jit(solution)/shard_map/ppermute | solution.py:222
  22.0 1.0 %shard_map.77 = f32[512,128]{1,0:T(8,128)} custom-call(bf16[512,128]{1,0:T(8,128)(2,1)S(1)} %bitcast.16, bf16[512,512]{1,0:T(8,128)(2,1)S(1)} %get-tuple-element.10.soft_ref, bf16[128,128]{1,0:T(8,128)(2,1)S(1)} %bitcast.13, bf16[128,256]{1,0:T(8,128)(2,1)S(1)} %collective-permute-done.rest_0_, bf16[128,256]{1,0:T(8,128)(2,1)S(1)} %collective-permute-done.1.rest_1_, ...), custom_call_target="tpu_custom_call" | custom-call | flops 67108864 | bytes 524288 | tf_op jit(solution)/shard_map/pallas_call | solution.py:223
  23.1 0.0 collective-permute-done.3.rest_0_
  23.1 0.5 %collective-permute-done.4.rest_1_ = bf16[128,256]{1,0:T(8,128)(2,1)S(1)} collective-permute-done((bf16[128,256]{1,0:T(8,128)(2,1)S(1)}, bf16[128,256]{1,0:T(8,128)(2,1)S(1)}, u32[]{:S(2)}, u32[]{:S(2)}) %collective-permute-start.4) | collective-permute-done | bytes 65568 | tf_op jit(solution)/shard_map/ppermute | solution.py:222
  23.5 2.5 %collective-permute-done.5.rest_2_ = bf16[128,256]{1,0:T(8,128)(2,1)S(1)} collective-permute-done((bf16[128,256]{1,0:T(8,128)(2,1)S(1)}, bf16[128,256]{1,0:T(8,128)(2,1)S(1)}, u32[]{:S(2)}, u32[]{:S(2)}) %collective-permute-start.5) | collective-permute-done | bytes 65568 | tf_op jit(solution)/shard_map/ppermute | solution.py:222
  26.1 0.7 %shard_map.78 = (f32[128,128]{1,0:T(8,128)}, f32[128,128]{1,0:T(8,128)}) custom-call(bf16[128,128]{1,0:T(8,128)(2,1)S(1)} %bitcast.14, bf16[128,128]{1,0:T(8,128)(2,1)S(1)} %bitcast.19, f32[128,256]{1,0:T(8,128)S(1)} %get-tuple-element.11.own_ref, bf16[128,256]{1,0:T(8,128)(2,1)S(1)} %collective-permute-done.3.rest_0_, ...), custom_call_target="tpu_custom_call" | custom-call | tf_op jit(solution)/shard_map/pallas_call | solution.py:235
Async XLA Ops:
  0.6 12.6 %copy-start = (bf16[1,128,128]{2,1,0:T(8,128)(2,1)S(1)}, bf16[1,128,128]{2,1,0:T(8,128)(2,1)}, u32[]{:S(2)}) copy-start(bf16[1,128,128]{2,1,0:T(8,128)(2,1)} %param.6) | copy-start | bytes 98308
  0.6 12.6 %copy-start.2 = (bf16[1,128,128]{2,1,0:T(8,128)(2,1)S(1)}, bf16[1,128,128]{2,1,0:T(8,128)(2,1)}, u32[]{:S(2)}) copy-start(bf16[1,128,128]{2,1,0:T(8,128)(2,1)} %param.7) | copy-start | bytes 98308
  1.5 5.8 %collective-permute-start = (bf16[128,256]{1,0:T(8,128)(2,1)S(1)}, bf16[128,256]{1,0:T(8,128)(2,1)S(1)}, u32[]{:S(2)}, u32[]{:S(2)}) collective-permute-start(bf16[128,256]{1,0:T(8,128)(2,1)S(1)} %pad_maximum_fusion), channel_id=1, source_target_pairs={{0,4},{4,0},{8,12},{12,8},{1,5},{5,1},{9,13},{13,9},{2,6},{6,2},{1... | collective-permute-start | bytes 196616 | tf_op jit(solution)/shard_map/ppermute | solution.py:197
  4.6 7.3 %collective-permute-start.1 = (bf16[128,256]{1,0:T(8,128)(2,1)S(1)}, bf16[128,256]{1,0:T(8,128)(2,1)S(1)}, u32[]{:S(2)}, u32[]{:S(2)}) collective-permute-start(bf16[128,256]{1,0:T(8,128)(2,1)S(1)} %pad_maximum_fusion), channel_id=1, source_target_pairs={{0,8},{4,12},{8,0},{12,4},{1,9},{5,13},{9,1},{13,5},{2,10},{6,14},... | collective-permute-start | bytes 196616 | tf_op jit(solution)/shard_map/ppermute | solution.py:197
  7.2 6.1 %collective-permute-start.2 = (bf16[128,256]{1,0:T(8,128)(2,1)S(1)}, bf16[128,256]{1,0:T(8,128)(2,1)S(1)}, u32[]{:S(2)}, u32[]{:S(2)}) collective-permute-start(bf16[128,256]{1,0:T(8,128)(2,1)S(1)} %pad_maximum_fusion), channel_id=1, source_target_pairs={{0,12},{4,8},{8,4},{12,0},{1,13},{5,9},{9,5},{13,1},{2,14},{6,10},... | collective-permute-start | bytes 196616 | tf_op jit(solution)/shard_map/ppermute | solution.py:197
  13.3 0.7 %copy-start.4 = (s32[8]{0:T(128)S(1)}, s32[8]{0:T(128)}, u32[]{:S(2)}) copy-start(s32[8]{0:T(128)} %order_ref.1) | copy-start | bytes 100
  13.9 0.9 %copy-start.1 = (bf16[4,128,128]{2,1,0:T(8,128)(2,1)S(1)}, bf16[4,128,128]{2,1,0:T(8,128)(2,1)}, u32[]{:S(2)}) copy-start(bf16[4,128,128]{2,1,0:T(8,128)(2,1)} %param.5) | copy-start | bytes 393220
  14.8 0.9 %copy-start.3 = (bf16[4,128,128]{2,1,0:T(8,128)(2,1)S(1)}, bf16[4,128,128]{2,1,0:T(8,128)(2,1)}, u32[]{:S(2)}) copy-start(bf16[4,128,128]{2,1,0:T(8,128)(2,1)} %param.8) | copy-start | bytes 393220
  17.6 5.5 %collective-permute-start.3 = (bf16[128,256]{1,0:T(8,128)(2,1)S(1)}, bf16[128,256]{1,0:T(8,128)(2,1)S(1)}, u32[]{:S(2)}, u32[]{:S(2)}) collective-permute-start(bf16[128,256]{1,0:T(8,128)(2,1)S(1)} %get-tuple-element.12), channel_id=1, source_target_pairs={{0,4},{4,0},{8,12},{12,8},{1,5},{5,1},{9,13},{13,9},{2,6},{6,2},{1... | collective-permute-start | bytes 196616 | tf_op jit(solution)/shard_map/ppermute | solution.py:222
  17.7 5.9 %collective-permute-start.4 = (bf16[128,256]{1,0:T(8,128)(2,1)S(1)}, bf16[128,256]{1,0:T(8,128)(2,1)S(1)}, u32[]{:S(2)}, u32[]{:S(2)}) collective-permute-start(bf16[128,256]{1,0:T(8,128)(2,1)S(1)} %get-tuple-element.13), channel_id=1, source_target_pairs={{0,8},{4,12},{8,0},{12,4},{1,9},{5,13},{9,1},{13,5},{2,10},{6,14},... | collective-permute-start | bytes 196616 | tf_op jit(solution)/shard_map/ppermute | solution.py:222
  20.0 6.1 %collective-permute-start.5 = (bf16[128,256]{1,0:T(8,128)(2,1)S(1)}, bf16[128,256]{1,0:T(8,128)(2,1)S(1)}, u32[]{:S(2)}, u32[]{:S(2)}) collective-permute-start(bf16[128,256]{1,0:T(8,128)(2,1)S(1)} %get-tuple-element.14), channel_id=1, source_target_pairs={{0,12},{4,8},{8,4},{12,0},{1,13},{5,9},{9,5},{13,1},{2,14},{6,10},... | collective-permute-start | bytes 196616 | tf_op jit(solution)/shard_map/ppermute | solution.py:222

commit v2 on v1

v2 whole, which is shorter than its diff:
```python
import functools
import math

import jax
import jax.numpy as jnp
from jax import lax
from jax.experimental import pallas as pl
from jax.experimental.pallas import tpu as pltpu
from jax.sharding import PartitionSpec as P


F32 = jnp.float32
BF16 = jnp.bfloat16
HIDDEN = -1e30
FEW = 8
LOG2E = math.log2(math.e)
KEYS_FIRST = (2, 3, 1)
TERMS_FIRST = (2, 3, 1)


def dot(a, b, dims):
    return lax.dot_general(a, b, (dims, ((), ())), preferred_element_type=F32)


def folded(combine, tile):
    return combine(tile.reshape(tile.shape[0] // 8, 8, tile.shape[1]), axis=0)


def masked_scores(blocks, block_rows, order_ref, mine, owner, query, keys):
    rows, queries = blocks * block_rows, query.shape[0]
    lane = lax.broadcasted_iota(jnp.int32, (1, queries), 1) % rows
    places = lane % block_rows
    for block in range(blocks):
        first = order_ref[mine * blocks + block] * block_rows
        places = places + jnp.where(lane // block_rows == block, first, 0)
    inner = lax.broadcasted_iota(jnp.int32, (block_rows, queries), 0)
    found = dot(keys, query, ((1,), (1,)))
    parts = []
    for block in range(blocks):
        first = order_ref[owner * blocks + block] * block_rows
        part = found[block * block_rows : (block + 1) * block_rows]
        parts.append(jnp.where(inner <= places - first, part, HIDDEN))
    return jnp.concatenate(parts, axis=0)


def block_softmax(blocks, block_rows, scale, slot, order_ref, owner_ref, query, ratio, both):
    head = query.shape[1]
    found = masked_scores(
        blocks, block_rows, order_ref, owner_ref[0], owner_ref[slot], query, both[:, :head]
    )
    top = jnp.max(folded(jnp.max, found), axis=0, keepdims=True)
    power = jnp.exp2((found - top) * (scale * LOG2E))
    grad = dot(both[:, head:], ratio, ((1,), (1,)))
    total = jnp.sum(folded(jnp.sum, power), axis=0, keepdims=True)
    weighted = jnp.sum(folded(jnp.sum, power * grad), axis=0, keepdims=True)
    return power, grad, (top, total, weighted)


def block_kernel(shape, scale, slot, order_ref, owner_ref, query_ref, ratio_ref, both_ref, power_ref, grad_ref, stat_ref):
    power, grad, stats = block_softmax(
        *shape, scale, slot, order_ref, owner_ref, query_ref[...], ratio_ref[...], both_ref[...]
    )
    power_ref[...] = power
    grad_ref[...] = grad
    for row, stat in enumerate(stats):
        stat_ref[row : row + 1, :] = stat


def finish(power, grad, share, expect, query, ratio):
    weights = power * share
    soft = (weights * (grad - expect)).astype(BF16)
    key_part = dot(soft, query, ((1,), (0,)))
    value_part = dot(weights.astype(BF16), ratio, ((1,), (0,)))
    return soft, key_part, value_part


def last_kernel(shape, scale, slot, others, order_ref, owner_ref, query_ref, ratio_ref, both_ref, *rest):
    *stat_refs, term_ref, soft_ref, norm_ref = rest
    head = query_ref.shape[1]
    query, ratio = query_ref[...], ratio_ref[...]
    power, grad, own_stats = block_softmax(
        *shape, scale, slot, order_ref, owner_ref, query, ratio, both_ref[...]
    )
    stats = {slot: own_stats}
    for other, ref in zip(others, stat_refs):
        stats[other] = (ref[0:1, :], ref[1:2, :], ref[2:3, :])
    top = functools.reduce(jnp.maximum, [stat[0] for stat in stats.values()])
    shares = {one: jnp.exp2((stat[0] - top) * (scale * LOG2E)) for one, stat in stats.items()}
    total = functools.reduce(jnp.add, [shares[one] * stats[one][1] for one in stats])
    weighted = functools.reduce(jnp.add, [shares[one] * stats[one][2] for one in stats])
    whole = 1.0 / total
    expect = weighted * whole
    for other in others:
        norm_ref[other : other + 1, :] = shares[other] * whole
    norm_ref[slot : slot + 1, :] = expect
    soft, key_part, value_part = finish(power, grad, shares[slot] * whole, expect, query, ratio)
    soft_ref[...] = soft
    term_ref[:, :head] = key_part.astype(BF16)
    term_ref[:, head:] = value_part.astype(BF16)


def term_kernel(slot, last, query_ref, ratio_ref, power_ref, grad_ref, norm_ref, term_ref, soft_ref):
    head = query_ref.shape[1]
    soft, key_part, value_part = finish(
        power_ref[...],
        grad_ref[...],
        norm_ref[slot : slot + 1, :],
        norm_ref[last : last + 1, :],
        query_ref[...],
        ratio_ref[...],
    )
    soft_ref[...] = soft
    term_ref[:, :head] = key_part.astype(term_ref.dtype)
    term_ref[:, head:] = value_part.astype(term_ref.dtype)


def own_kernel(factor, last, query_ref, ratio_ref, power_ref, grad_ref, norm_ref, both_ref, *rest):
    *pairs, own_ref, out_ref = rest
    head = query_ref.shape[1]
    soft, key_part, value_part = finish(
        power_ref[...],
        grad_ref[...],
        norm_ref[0:1, :],
        norm_ref[last : last + 1, :],
        query_ref[...],
        ratio_ref[...],
    )
    own_ref[:, :head] = key_part
    own_ref[:, head:] = value_part
    found = dot(soft, both_ref[:, :head], ((0,), (0,)))
    for soft_ref, seen_ref in zip(pairs[::2], pairs[1::2]):
        found += dot(soft_ref[...], seen_ref[:, :head], ((0,), (0,)))
    out_ref[...] = factor * query_ref[...].astype(F32) * found


def sum_kernel(factor, both_ref, own_ref, *rest):
    *got, key_out, value_out = rest
    head = key_out.shape[1]
    total = own_ref[...]
    for one in got:
        total = total + one[...].astype(F32)
    key_out[...] = factor * both_ref[:, :head].astype(F32) * total[:, :head]
    value_out[...] = both_ref[:, head:].astype(F32) * total[:, head:]


def whole_kernel(shape, scale, order_ref, owner_ref, query_ref, ratio_ref, seen_ref, terms_ref, out_ref, score_ref, grad_ref):
    slots, blocks, block_rows = shape
    rows = blocks * block_rows
    queries, head = query_ref.shape
    query, ratio = query_ref[...], ratio_ref[...]

    def rows_of(slot):
        return pl.ds(pl.multiple_of(slot * rows, rows), rows)

    def scores(slot, top):
        found = masked_scores(
            blocks, block_rows, order_ref, owner_ref[0], slot, query, seen_ref[slot, :, :head]
        )
        score_ref[rows_of(slot), :] = found
        grad_ref[rows_of(slot), :] = dot(seen_ref[slot, :, head:], ratio, ((1,), (1,)))
        return jnp.maximum(top, folded(jnp.max, found))

    top = lax.fori_loop(0, slots, scores, jnp.full((8, queries), HIDDEN, F32))
    top = jnp.max(top, axis=0, keepdims=True)
    zero = jnp.zeros((8, queries), F32)

    def exps(slot, sums):
        power = jnp.exp2((score_ref[rows_of(slot), :] - top) * (scale * LOG2E))
        score_ref[rows_of(slot), :] = power
        weighted = power * grad_ref[rows_of(slot), :]
        return sums[0] + folded(jnp.sum, power), sums[1] + folded(jnp.sum, weighted)

    total, weighted = lax.fori_loop(0, slots, exps, (zero, zero))
    share = 1.0 / jnp.sum(total, axis=0, keepdims=True)
    expect = jnp.sum(weighted, axis=0, keepdims=True) * share
    out_ref[...] = jnp.zeros_like(out_ref)

    def terms(slot, carry):
        soft, key_part, value_part = finish(
            score_ref[rows_of(slot), :], grad_ref[rows_of(slot), :], share, expect, query, ratio
        )
        terms_ref[slot, :, :head] = key_part
        terms_ref[slot, :, head:] = value_part
        out_ref[...] += dot(soft, seen_ref[slot, :, :head], ((0,), (0,)))
        return carry

    lax.fori_loop(0, slots, terms, 0)
    out_ref[...] = 0.5 * scale * query.astype(F32) * out_ref[...]


def body(query, keys, values, ratio, block_order):
    kv_heads, rows, head = keys.shape
    group = query.shape[0] // kv_heads
    queries = group * rows
    scale = head ** (-0.5)
    slots = lax.axis_size("seq")
    mine = lax.axis_index("seq")
    blocks = block_order.shape[0] // slots
    block_rows = rows // blocks
    shape = (blocks, block_rows)
    swap = slots & (slots - 1) == 0
    limit = min(60 << 20, (8 << 20) + 16 * slots * rows * queries)
    params = pltpu.CompilerParams(vmem_limit_bytes=limit)
    smem = pl.BlockSpec(memory_space=pltpu.SMEM)
    vmem = pl.BlockSpec(memory_space=pltpu.VMEM)
    tile = jax.ShapeDtypeStruct((rows, queries), F32)
    low_tile = jax.ShapeDtypeStruct((rows, queries), BF16)
    stat = jax.ShapeDtypeStruct((8, queries), F32)
    low_term = jax.ShapeDtypeStruct((rows, 2 * head), BF16)
    term = jax.ShapeDtypeStruct((rows, 2 * head), F32)
    part = jax.ShapeDtypeStruct((rows, head), F32)
    rel = jax.ShapeDtypeStruct((queries, head), F32)

    def run(kernel, outs, scalars, arrays, dots, scratch=()):
        single = not isinstance(outs, tuple)
        return pl.pallas_call(
            kernel,
            out_shape=outs,
            in_specs=[smem] * len(scalars) + [vmem] * len(arrays),
            out_specs=vmem if single else (vmem,) * len(outs),
            scratch_shapes=scratch,
            compiler_params=params,
            cost_estimate=pl.CostEstimate(
                flops=2 * dots * rows * queries * head,
                bytes_accessed=4 * dots * rows * queries,
                transcendentals=rows * queries,
            ),
        )(*scalars, *arrays)

    def pairs(step, back):
        if swap:
            return [(device, device ^ step) for device in range(slots)]
        step = -step if back else step
        return [(device, (device + step) % slots) for device in range(slots)]

    def many(query_rows, ratio_rows, both):
        seen = lax.all_gather(both, "seq")
        terms, query_out = run(
            functools.partial(whole_kernel, (slots, *shape), scale),
            (jax.ShapeDtypeStruct((slots, rows, 2 * head), F32), rel),
            (block_order, mine.reshape(1)),
            (query_rows, ratio_rows, seen),
            5 * slots,
            [pltpu.VMEM((slots * rows, queries), F32)] * 2,
        )
        own = lax.psum_scatter(terms, "seq", scatter_dimension=0, tiled=False)
        return own, [], query_out

    def few(query_rows, ratio_rows, both):
        steps = range(1, slots)
        first = KEYS_FIRST if slots == len(KEYS_FIRST) + 1 else tuple(steps)
        then = TERMS_FIRST if slots == len(TERMS_FIRST) + 1 else tuple(steps)
        last = then[0]
        others = [slot for slot in (0, *first) if slot != last]
        seen = {0: both}
        for step in first:
            seen[step] = lax.ppermute(both, "seq", pairs(step, False))
        device = jnp.arange(slots, dtype=jnp.int32)
        owners = mine ^ device if swap else lax.rem(mine - device + slots, slots)
        power, grad, stats = {}, {}, {}
        for slot in others:
            power[slot], grad[slot], stats[slot] = run(
                functools.partial(block_kernel, shape, scale, slot),
                (tile, tile, stat),
                (block_order, owners),
                (query_rows, ratio_rows, seen[slot]),
                2,
            )
        terms, soft, got = {}, {}, {}
        for slot in then:
            if slot == last:
                terms[slot], soft[slot], norm = run(
                    functools.partial(last_kernel, shape, scale, slot, others),
                    (low_term, low_tile, stat),
                    (block_order, owners),
                    (query_rows, ratio_rows, seen[slot], *(stats[one] for one in others)),
                    4,
                )
            else:
                terms[slot], soft[slot] = run(
                    functools.partial(term_kernel, slot, last),
                    (low_term, low_tile),
                    (),
                    (query_rows, ratio_rows, power[slot], grad[slot], norm),
                    2,
                )
            got[slot] = lax.ppermute(terms[slot], "seq", pairs(slot, True))
        own, query_out = run(
            functools.partial(own_kernel, 0.5 * scale, last),
            (term, rel),
            (),
            (
                *(query_rows, ratio_rows, power[0], grad[0], norm, both),
                *(one for slot in steps for one in (soft[slot], seen[slot])),
            ),
            2 + slots,
        )
        return own, list(got.values()), query_out

    def one_head(query_rows, ratio_rows, key_rows, value_rows):
        both = jnp.concatenate((key_rows, value_rows), axis=1)
        own, got, query_out = (many if slots > FEW else few)(query_rows, ratio_rows, both)
        key_out, value_out = run(
            functools.partial(sum_kernel, 0.5 * scale), (part, part), (), (both, own, *got), 0
        )
        return query_out.reshape(group, rows, head), key_out, value_out

    results = [
        one_head(
            query[g * group : (g + 1) * group].reshape(queries, head),
            ratio[g * group : (g + 1) * group].reshape(queries, head),
            keys[g],
            values[g],
        )
        for g in range(kv_heads)
    ]
    return (
        jnp.concatenate([one for one, _, _ in results], axis=0),
        jnp.stack([one for _, one, _ in results], axis=0),
        jnp.stack([one for _, _, one in results], axis=0),
    )


def solution(mesh):
    spec = P("head", ("groups", "seq"), None)
    return jax.shard_map(
        body,
        mesh=mesh,
        in_specs=(spec, spec, spec, spec, P("groups")),
        out_specs=(spec, spec, spec),
        check_vma=False,
    )
```

time: 27 us -> 24.3 us (0.900)
  waiting for transfers between devices: 8.96 us -> 5.97 us
  Pallas kernels: 3.57 us -> 5.7 us
  local copies, waits for them, and re-layouts: 2.55 us -> 1.56 us
  starting transfers between devices: 10.2 us -> 9.39 us
    ppermute x6, waiting for transfers between devices: 8.96 us -> 5.97 us  [the longest x3 3.67 us: few(): got[slot] = lax.ppermute(terms[slot], 'seq', pairs(slot, True))]
    pallas_call x3 -> x8, Pallas kernels: 3.57 us -> 5.7 us  [run(): pl.pallas_call(kernel, out_shape=outs, in_specs=[smem] * len(scalars) + [...]
    unnamed x10 -> x6, local copies, waits for them, and re-layouts: 2.47 us -> 1.56 us
    ppermute x6, starting transfers between devices: 10.2 us -> 9.39 us  [the longest x3 5.7 us: few(): seen[step] = lax.ppermute(both, 'seq', pairs(step, False))]
  transfers between devices with their start and end apart: 6 -> 6, of which waited for: 4 -> 4; matrix products, arithmetic and copies ran while one was open for 0% -> 0% of each run, Pallas kernels for 4% -> 17%
where the time goes in v2:
time: 24.3 us; the launch traced here: 24.1 us
  starting transfers between devices  9.39 us (39%)
  waiting for transfers between devices  5.97 us (25%)
  Pallas kernels  5.7 us (23%)
  local copies, waits for them, and re-layouts  1.56 us (6%)
  other arithmetic  0.82 us (3%)
  between operations  0.7 us (3%)
    ppermute x3, starting transfers between devices, few(): seen[step] = lax.ppermute(both, 'seq', pairs(step, False))  5.7 us
    pallas_call x8, Pallas kernels, run(): pl.pallas_call(kernel, out_shape=outs, in_specs=[smem] * len(scalars) + [...  5.7 us
    ppermute x3, starting transfers between devices, few(): got[slot] = lax.ppermute(terms[slot], 'seq', pairs(slot, True))  3.68 us
    ppermute x3, waiting for transfers between devices, few(): got[slot] = lax.ppermute(terms[slot], 'seq', pairs(slot, True))  3.67 us
    ppermute x3, waiting for transfers between devices, few(): seen[step] = lax.ppermute(both, 'seq', pairs(step, False))  2.3 us
    unnamed x6, local copies, waits for them, and re-layouts  1.56 us
    concatenate x1, other arithmetic, one_head(): both = jnp.concatenate((key_rows, value_rows), axis=1)  0.82 us
  transfers between devices with their start and end apart: 6, of which 4 were waited for; matrix products, arithmetic and copies ran while one was open for 0% of the time, Pallas kernels for 17%

profile of v2, /device:TPU:0, one launch (start us, length us, event | category | flops | bytes accessed | tf_op | source)
XLA Modules:
  0.0 24.1 jit_solution(1025953641319881317)
XLA Ops:
  0.6 0.0 copy-start
  0.6 0.8 %pad_maximum_fusion.both_ref = bf16[128,256]{1,0:T(8,128)(2,1)S(1)} fusion(bf16[128,128]{1,0:T(8,128)(2,1)} %bitcast.21, bf16[128,128]{1,0:T(8,128)(2,1)} %bitcast.22), kind=kLoop, calls=%fused_computation | loop fusion | flops 131072 | bytes 131072 | tf_op jit(solution)/shard_map/concatenate | solution.py:301
  1.5 3.1 %collective-permute-start.2 = (bf16[128,256]{1,0:T(8,128)(2,1)S(1)}, bf16[128,256]{1,0:T(8,128)(2,1)S(1)}, u32[]{:S(2)}, u32[]{:S(2)}) collective-permute-start(bf16[128,256]{1,0:T(8,128)(2,1)S(1)} %pad_maximum_fusion.both_ref), channel_id=1, source_target_pairs={{0,4},{4,0},{8,12},{12,8},{1,5},{5,1},{9,13},{13,9},{2,6},{6,2},{1... | collective-permute-start | bytes 196616 | tf_op jit(solution)/shard_map/ppermute | solution.py:257
  4.6 2.5 %collective-permute-start.1 = (bf16[128,256]{1,0:T(8,128)(2,1)S(1)}, bf16[128,256]{1,0:T(8,128)(2,1)S(1)}, u32[]{:S(2)}, u32[]{:S(2)}) collective-permute-start(bf16[128,256]{1,0:T(8,128)(2,1)S(1)} %pad_maximum_fusion.both_ref), channel_id=1, source_target_pairs={{0,12},{4,8},{8,4},{12,0},{1,13},{5,9},{9,5},{13,1},{2,14},{6,10},... | collective-permute-start | bytes 196616 | tf_op jit(solution)/shard_map/ppermute | solution.py:257
  7.0 0.1 collective-permute-start
  7.2 0.0 copy-start.2
  7.2 0.0 copy-done
  7.2 0.7 %copy-done.2 = s32[8]{0:T(128)S(1)} copy-done((s32[8]{0:T(128)S(1)}, s32[8]{0:T(128)}, u32[]{:S(2)}) %copy-start.2) | copy-done | bytes 56
  7.8 0.0 copy-start.1
  7.8 0.9 %copy-done.1 = bf16[4,128,128]{2,1,0:T(8,128)(2,1)S(1)} copy-done((bf16[4,128,128]{2,1,0:T(8,128)(2,1)S(1)}, bf16[4,128,128]{2,1,0:T(8,128)(2,1)}, u32[]{:S(2)}) %copy-start.1) | copy-done | bytes 131096
  8.7 0.8 %shard_map.76 = (f32[128,512]{1,0:T(8,128)S(1)}, f32[128,512]{1,0:T(8,128)S(1)}, f32[8,512]{1,0:T(8,128)S(1)}) custom-call(s32[8]{0:T(128)S(1)} %copy-done.2, s32[4]{0:T(128)S(1)} %iota_xor_fusion.owner_ref, bf16[512,128]{1,0:T(8,128)(2,1)S(1)} %bitcast.7, bf16[512,128]{1,0:T(8,128)(2,1)S(1)} %bitcast.14, bf16[128,256]{1,0:T(8,128)(2,1)S(1)} %pad_maximum_fusion.both_ref), custom_call_target="tpu_custom_call" | custom-call | flops 33554432 | bytes 524288 | tf_op jit(solution)/shard_map/pallas_call | solution.py:216
  9.5 1.9 %collective-permute-done.1.both_ref.rest_5_ = bf16[128,256]{1,0:T(8,128)(2,1)S(1)} collective-permute-done((bf16[128,256]{1,0:T(8,128)(2,1)S(1)}, bf16[128,256]{1,0:T(8,128)(2,1)S(1)}, u32[]{:S(2)}, u32[]{:S(2)}) %collective-permute-start.1) | collective-permute-done | bytes 65568 | tf_op jit(solution)/shard_map/ppermute | solution.py:257
  11.4 0.8 %shard_map.77 = (f32[128,512]{1,0:T(8,128)S(1)}, f32[128,512]{1,0:T(8,128)S(1)}, f32[8,512]{1,0:T(8,128)S(1)}) custom-call(s32[8]{0:T(128)S(1)} %copy-done.2, s32[4]{0:T(128)S(1)} %iota_xor_fusion.owner_ref, bf16[512,128]{1,0:T(8,128)(2,1)S(1)} %bitcast.8, bf16[512,128]{1,0:T(8,128)(2,1)S(1)} %bitcast.15, ...), custom_call_target="tpu_custom_call" | custom-call | flops 33554432 | bytes 524288 | tf_op jit(solution)/shard_map/pallas_call | solution.py:216
  12.3 0.0 collective-permute-done.2.both_ref.rest_1_
  12.3 0.8 %shard_map.78 = (f32[128,512]{1,0:T(8,128)S(1)}, f32[128,512]{1,0:T(8,128)S(1)}, f32[8,512]{1,0:T(8,128)S(1)}) custom-call(s32[8]{0:T(128)S(1)} %copy-done.2, s32[4]{0:T(128)S(1)} %iota_xor_fusion.owner_ref, bf16[512,128]{1,0:T(8,128)(2,1)S(1)} %bitcast.9, bf16[512,128]{1,0:T(8,128)(2,1)S(1)} %bitcast.16, ...), custom_call_target="tpu_custom_call" | custom-call | flops 33554432 | bytes 524288 | tf_op jit(solution)/shard_map/pallas_call | solution.py:216
  13.1 0.4 %collective-permute-done.both_ref.rest_3_ = bf16[128,256]{1,0:T(8,128)(2,1)S(1)} collective-permute-done((bf16[128,256]{1,0:T(8,128)(2,1)S(1)}, bf16[128,256]{1,0:T(8,128)(2,1)S(1)}, u32[]{:S(2)}, u32[]{:S(2)}) %collective-permute-start) | collective-permute-done | bytes 65568 | tf_op jit(solution)/shard_map/ppermute | solution.py:257
  13.5 1.0 %shard_map.79 = (bf16[128,256]{1,0:T(8,128)(2,1)S(1)}, bf16[128,512]{1,0:T(8,128)(2,1)S(1)}, f32[8,512]{1,0:T(8,128)S(1)}) custom-call(s32[8]{0:T(128)S(1)} %copy-done.2, s32[4]{0:T(128)S(1)} %iota_xor_fusion.owner_ref, bf16[512,128]{1,0:T(8,128)(2,1)S(1)} %bitcast.10, bf16[512,128]{1,0:T(8,128)(2,1)S(1)} %bitcast.17, ...), custom_call_target="tpu_custom_call" | custom-call | flops 67108864 | bytes 1048576 | tf_op jit(solution)/shard_map/pallas_call | solution.py:216
  14.5 2.5 %collective-permute-start.3 = (bf16[128,256]{1,0:T(8,128)(2,1)S(1)}, bf16[128,256]{1,0:T(8,128)(2,1)S(1)}, u32[]{:S(2)}, u32[]{:S(2)}) collective-permute-start(bf16[128,256]{1,0:T(8,128)(2,1)S(1)} %get-tuple-element.38), channel_id=1, source_target_pairs={{0,8},{4,12},{8,0},{12,4},{1,9},{5,13},{9,1},{13,5},{2,10},{6,14},... | collective-permute-start | bytes 196616 | tf_op jit(solution)/shard_map/ppermute | solution.py:287
  17.1 0.2 shard_map.81
  17.3 0.5 %collective-permute-start.4 = (bf16[128,256]{1,0:T(8,128)(2,1)S(1)}, bf16[128,256]{1,0:T(8,128)(2,1)S(1)}, u32[]{:S(2)}, u32[]{:S(2)}) collective-permute-start(bf16[128,256]{1,0:T(8,128)(2,1)S(1)} %get-tuple-element.39), channel_id=1, source_target_pairs={{0,12},{4,8},{8,4},{12,0},{1,13},{5,9},{9,5},{13,1},{2,14},{6,10},... | collective-permute-start | bytes 196616 | tf_op jit(solution)/shard_map/ppermute | solution.py:287
  17.9 0.2 shard_map.80
  18.1 0.6 %collective-permute-start.5 = (bf16[128,256]{1,0:T(8,128)(2,1)S(1)}, bf16[128,256]{1,0:T(8,128)(2,1)S(1)}, u32[]{:S(2)}, u32[]{:S(2)}) collective-permute-start(bf16[128,256]{1,0:T(8,128)(2,1)S(1)} %get-tuple-element.40), channel_id=1, source_target_pairs={{0,4},{4,0},{8,12},{12,8},{1,5},{5,1},{9,13},{13,9},{2,6},{6,2},{1... | collective-permute-start | bytes 196616 | tf_op jit(solution)/shard_map/ppermute | solution.py:287
  18.7 1.1 %shard_map.82 = (f32[128,256]{1,0:T(8,128)S(1)}, f32[512,128]{1,0:T(8,128)}) custom-call(bf16[512,128]{1,0:T(8,128)(2,1)S(1)} %bitcast.13, bf16[512,128]{1,0:T(8,128)(2,1)S(1)} %bitcast.20, f32[128,512]{1,0:T(8,128)S(1)} %get-tuple-element.23.power_ref, f32[128,512]{1,0:T(8,128)S(1)} %get-tuple-element.24.grad_ref, f32[8,512]{1,0:T(8,128)S(1)} %get-tuple-element.28.norm_ref, ...), custom_call_target="tpu_custom_call" | custom-call | flops 100663296 | bytes 1572864 | tf_op jit(solution)/shard_map/pallas_call | solution.py:216
  19.8 1.8 %collective-permute-done.3.rest_0_ = bf16[128,256]{1,0:T(8,128)(2,1)S(1)} collective-permute-done((bf16[128,256]{1,0:T(8,128)(2,1)S(1)}, bf16[128,256]{1,0:T(8,128)(2,1)S(1)}, u32[]{:S(2)}, u32[]{:S(2)}) %collective-permute-start.3) | collective-permute-done | bytes 65568 | tf_op jit(solution)/shard_map/ppermute | solution.py:287
  21.6 1.9 %collective-permute-done.4.rest_1_ = bf16[128,256]{1,0:T(8,128)(2,1)S(1)} collective-permute-done((bf16[128,256]{1,0:T(8,128)(2,1)S(1)}, bf16[128,256]{1,0:T(8,128)(2,1)S(1)}, u32[]{:S(2)}, u32[]{:S(2)}) %collective-permute-start.4) | collective-permute-done | bytes 65568 | tf_op jit(solution)/shard_map/ppermute | solution.py:287
  23.5 0.0 collective-permute-done.5.rest_2_
  23.5 0.7 %shard_map.83 = (f32[128,128]{1,0:T(8,128)}, f32[128,128]{1,0:T(8,128)}) custom-call(bf16[128,256]{1,0:T(8,128)(2,1)S(1)} %pad_maximum_fusion.both_ref, f32[128,256]{1,0:T(8,128)S(1)} %get-tuple-element.37.own_ref, bf16[128,256]{1,0:T(8,128)(2,1)S(1)} %collective-permute-done.3.rest_0_, bf16[128,256]{1,0:T(8,128)(2,1)S(1)} %collective-permute-done.4.rest_1_, ...), custom_call_target="tpu_custom_call" | custom-call | tf_op jit(solution)/shard_map/pallas_call | solution.py:216
  (1 shorter events, 0.0 us)
Async XLA Ops:
  0.6 6.5 %copy-start = (bf16[4,128,128]{2,1,0:T(8,128)(2,1)S(1)}, bf16[4,128,128]{2,1,0:T(8,128)(2,1)}, u32[]{:S(2)}) copy-start(bf16[4,128,128]{2,1,0:T(8,128)(2,1)} %param.5) | copy-start | bytes 393220
  1.5 10.8 %collective-permute-start.2 = (bf16[128,256]{1,0:T(8,128)(2,1)S(1)}, bf16[128,256]{1,0:T(8,128)(2,1)S(1)}, u32[]{:S(2)}, u32[]{:S(2)}) collective-permute-start(bf16[128,256]{1,0:T(8,128)(2,1)S(1)} %pad_maximum_fusion.both_ref), channel_id=1, source_target_pairs={{0,4},{4,0},{8,12},{12,8},{1,5},{5,1},{9,13},{13,9},{2,6},{6,2},{1... | collective-permute-start | bytes 196616 | tf_op jit(solution)/shard_map/ppermute | solution.py:257
  4.6 6.9 %collective-permute-start.1 = (bf16[128,256]{1,0:T(8,128)(2,1)S(1)}, bf16[128,256]{1,0:T(8,128)(2,1)S(1)}, u32[]{:S(2)}, u32[]{:S(2)}) collective-permute-start(bf16[128,256]{1,0:T(8,128)(2,1)S(1)} %pad_maximum_fusion.both_ref), channel_id=1, source_target_pairs={{0,12},{4,8},{8,4},{12,0},{1,13},{5,9},{9,5},{13,1},{2,14},{6,10},... | collective-permute-start | bytes 196616 | tf_op jit(solution)/shard_map/ppermute | solution.py:257
  7.0 6.4 %collective-permute-start = (bf16[128,256]{1,0:T(8,128)(2,1)S(1)}, bf16[128,256]{1,0:T(8,128)(2,1)S(1)}, u32[]{:S(2)}, u32[]{:S(2)}) collective-permute-start(bf16[128,256]{1,0:T(8,128)(2,1)S(1)} %pad_maximum_fusion.both_ref), channel_id=1, source_target_pairs={{0,8},{4,12},{8,0},{12,4},{1,9},{5,13},{9,1},{13,5},{2,10},{6,14},... | collective-permute-start | bytes 196616 | tf_op jit(solution)/shard_map/ppermute | solution.py:257
  7.2 0.7 %copy-start.2 = (s32[8]{0:T(128)S(1)}, s32[8]{0:T(128)}, u32[]{:S(2)}) copy-start(s32[8]{0:T(128)} %order_ref.7) | copy-start | bytes 100
  7.8 0.9 %copy-start.1 = (bf16[4,128,128]{2,1,0:T(8,128)(2,1)S(1)}, bf16[4,128,128]{2,1,0:T(8,128)(2,1)}, u32[]{:S(2)}) copy-start(bf16[4,128,128]{2,1,0:T(8,128)(2,1)} %param.8) | copy-start | bytes 393220
  14.5 7.0 %collective-permute-start.3 = (bf16[128,256]{1,0:T(8,128)(2,1)S(1)}, bf16[128,256]{1,0:T(8,128)(2,1)S(1)}, u32[]{:S(2)}, u32[]{:S(2)}) collective-permute-start(bf16[128,256]{1,0:T(8,128)(2,1)S(1)} %get-tuple-element.38), channel_id=1, source_target_pairs={{0,8},{4,12},{8,0},{12,4},{1,9},{5,13},{9,1},{13,5},{2,10},{6,14},... | collective-permute-start | bytes 196616 | tf_op jit(solution)/shard_map/ppermute | solution.py:287
  17.3 6.1 %collective-permute-start.4 = (bf16[128,256]{1,0:T(8,128)(2,1)S(1)}, bf16[128,256]{1,0:T(8,128)(2,1)S(1)}, u32[]{:S(2)}, u32[]{:S(2)}) collective-permute-start(bf16[128,256]{1,0:T(8,128)(2,1)S(1)} %get-tuple-element.39), channel_id=1, source_target_pairs={{0,12},{4,8},{8,4},{12,0},{1,13},{5,9},{9,5},{13,1},{2,14},{6,10},... | collective-permute-start | bytes 196616 | tf_op jit(solution)/shard_map/ppermute | solution.py:287
  18.1 5.4 %collective-permute-start.5 = (bf16[128,256]{1,0:T(8,128)(2,1)S(1)}, bf16[128,256]{1,0:T(8,128)(2,1)S(1)}, u32[]{:S(2)}, u32[]{:S(2)}) collective-permute-start(bf16[128,256]{1,0:T(8,128)(2,1)S(1)} %get-tuple-element.40), channel_id=1, source_target_pairs={{0,4},{4,0},{8,12},{12,8},{1,5},{5,1},{9,13},{13,9},{2,6},{6,2},{1... | collective-permute-start | bytes 196616 | tf_op jit(solution)/shard_map/ppermute | solution.py:287
